TPU v7x, 256 devices: a whole 4x4x8 slice. The times are simulated.
256 devices in a mesh: ctx: 64 (over x, z, core), tp: 4 (over y).
Axes of the slice: x: 4, y: 4, z: 8, core: 2. Of those that a mesh axis runs over, the one named last changes fastest.
Arguments:
- streams: bfloat16 [10240, 3, 4096], P('ctx', None, 'tp'), may hold values from -6 to 6
- short_taps: float32 [7, 3, 4096], P(None, None, 'tp'), may hold values from -2 to 2
- mix_taps: float32 [128, 4096], P(None, 'tp'), may hold values from -0.5 to 0.5
- pole_rate: float32 [16, 4096], P(None, 'tp'), may hold values from 9.765625e-06 to 0.06, as said below
- pole_angle: float32 [16, 4096], P(None, 'tp'), may hold values from -3.140625 to 3.140625
- residue: float32 [2, 16, 4096], P(None, None, 'tp'), may hold values from -1.5 to 1.5
- skip: float32 [4096], P('tp'), may hold values from -3 to 3
- out_weight: bfloat16 [4096, 4096], P('tp', 'ctx'), may hold values from -0.25 to 0.25
Outputs:
- mixed: bfloat16 [10240, 4096], P('ctx', 'tp')
Inputs may be any that keep to these rules, and one draw needn't show every extreme that they name: `pole_rate`: each pole's decay rate is positive.
All inputs are finite; a program needn't handle non-finite values.
Results may differ from a plain program's by a relative error of at most 0.0057.
Values may be sent and summed in bfloat16 or wider, within the bound.
A program may use at most 64 MiB of HBM per device.

v0:
```python
import jax
import jax.numpy as jnp
from jax import lax
from jax.sharding import PartitionSpec as P


def from_behind(block, axis, distance):
    devices = range(lax.axis_size(axis))
    route = [(i - distance, i) for i in devices if i - distance in devices]
    return lax.ppermute(block, axis, route)


def depthwise(ext, taps):
    width = taps.shape[1]
    kernel = taps[::-1][:, None, :]
    out = lax.conv_general_dilated(
        ext[None],
        kernel,
        (1,),
        "VALID",
        dimension_numbers=("NWC", "WIO", "NWC"),
        feature_group_count=width,
        precision=lax.Precision.HIGHEST,
    )
    return out[0]


def body(streams, short_taps, mix_taps, pole_rate, pole_angle, residue, skip, out_weight):
    rows, three, width = streams.shape
    modes = pole_rate.shape[0]
    short = short_taps.reshape(7, three * width)
    rim = from_behind(streams[rows - 6 :], "ctx", 1)
    ext = jnp.concatenate([rim, streams], 0).astype(jnp.float32).reshape(rows + 6, three * width)
    conv = depthwise(ext, short).reshape(rows, three, width)
    gate = (conv[:, 1] * conv[:, 2]).astype(jnp.bfloat16)
    gate_rim = from_behind(gate[rows - 127 :], "ctx", 1)
    gate_ext = jnp.concatenate([gate_rim, gate], 0)
    query = conv[:, 0]
    medium = depthwise(gate_ext.astype(jnp.float32), mix_taps)
    amp = jnp.sqrt(1.0 - jnp.exp(-2.0 * pole_rate))
    res_re = residue[0] * amp
    res_im = residue[1] * amp
    steps = jnp.arange(rows).astype(jnp.float32)[:, None]
    flipped = medium[::-1]

    def first_pass(mode, carry):
        filt, end_re, end_im = carry
        rate = pole_rate[mode][None]
        angle = pole_angle[mode][None]
        mag = jnp.exp(-rate * steps)
        cosk = mag * jnp.cos(angle * steps)
        sink = mag * jnp.sin(angle * steps)
        filt = filt + res_re[mode][None] * cosk - res_im[mode][None] * sink
        end_re = end_re.at[mode].set(jnp.sum(flipped * cosk, 0))
        end_im = end_im.at[mode].set(jnp.sum(flipped * sink, 0))
        return (filt, end_re, end_im)

    zero_state = jnp.zeros((modes, width), jnp.float32)
    filt, end_re, end_im = lax.fori_loop(
        0, modes, first_pass, (jnp.zeros((rows, width), jnp.float32), zero_state, zero_state)
    )
    dec_mag = jnp.exp(-pole_rate * rows)
    dec_re = dec_mag * jnp.cos(pole_angle * rows)
    dec_im = dec_mag * jnp.sin(pole_angle * rows)

    def relay_step(turn, received):
        in_re, in_im = received
        out_re = dec_re * in_re - dec_im * in_im + end_re
        out_im = dec_re * in_im + dec_im * in_re + end_im
        return from_behind((out_re, out_im), "ctx", 1)

    st_re, st_im = lax.fori_loop(0, lax.axis_size("ctx") - 1, relay_step, (zero_state, zero_state))
    later = steps + 1.0

    def second_pass(mode, inflow):
        rate = pole_rate[mode][None]
        angle = pole_angle[mode][None]
        mag = jnp.exp(-rate * later)
        cos1 = mag * jnp.cos(angle * later)
        sin1 = mag * jnp.sin(angle * later)
        are = res_re[mode] * st_re[mode] - res_im[mode] * st_im[mode]
        aim = res_re[mode] * st_im[mode] + res_im[mode] * st_re[mode]
        return inflow + are[None] * cos1 - aim[None] * sin1

    inflow = lax.fori_loop(0, modes, second_pass, jnp.zeros((rows, width), jnp.float32))
    padded = jnp.concatenate([jnp.zeros((rows - 1, width), jnp.float32), medium], 0)
    intra = depthwise(padded, filt)
    longf = intra + inflow + skip[None] * medium
    hidden = (query * longf).astype(jnp.bfloat16)
    partial_out = jnp.dot(
        hidden,
        lax.all_gather(out_weight, "ctx", axis=1, tiled=True),
        preferred_element_type=jnp.float32,
    )
    return lax.psum_scatter(partial_out, "tp", scatter_dimension=1, tiled=True).astype(jnp.bfloat16)


def solution(mesh):
    return jax.shard_map(
        body,
        mesh=mesh,
        in_specs=(
            P("ctx", None, "tp"),
            P(None, None, "tp"),
            P(None, "tp"),
            P(None, "tp"),
            P(None, "tp"),
            P(None, None, "tp"),
            P("tp"),
            P("tp", "ctx"),
        ),
        out_specs=P("ctx", "tp"),
        check_vma=False,
    )
```

profile of v0, /device:TPU:1, one launch (start us, length us, event | category | flops | bytes accessed | tf_op | source)
XLA Modules:
  0.0 879.0 jit_solution(4018767467548928476)
XLA Ops:
  7.4 4.9 collective-permute-start.2
  12.3 8.4 rev.12
  44.4 7.0 fusion.22
  54.0 94.6 %while.49 = (s32[]{:T(128)}, f32[160,1024]{1,0:T(8,128)S(1)}, f32[16,1024]{1,0:T(8,128)S(1)}, f32[16,1024]{1,0:T(8,128)S(1)}, f32[16,1024]{1,0:T(8,128)}, /*inde...) while((s32[]{:T(128)}, f32[160,1024]{1,0:T(8,128)S(1)}, ...), condition=%wide.region_4.5_spmd.clone.clone, body=%wide.region_0.4_spmd.clone.clone.sunk | while | flops 2131116 | bytes 2065845 | solution.py:59
  148.6 5.2 rev.15
  153.8 9.6 %fusion.20 = f32[1,160,1024]{2,0,1:T(1,128)S(1)} fusion(f32[1,319,1024]{2,1,0:T(8,128)} %pad_bitcast_fusion, f32[160,1,1024]{2,0,1:T(8,128)} %bitcast.84), kind=kOutput, calls=%fused_computation.43 | convolution fusion | flops 314572800 | bytes 2617344 | tf_op jit(solution)/shard_map/conv_general_dilated | solution.py:16
  163.4 586.5 %while.48 = (s32[]{:T(128)}, f32[16,1024]{1,0:T(8,128)S(1)}, f32[16,1024]{1,0:T(8,128)S(1)}, f32[16,1024]{1,0:T(8,128)S(1)}, f32[16,1024]{1,0:T(8,128)S(1)}, /*i...) while((s32[]{:T(128)}, f32[16,1024]{1,0:T(8,128)S(1)}, f32[16,1024]{1,0:T(8,128)S(1)}, ...), condition=%wide.region_6.0_spmd, body=%wide.region_5.0_spmd.sunk | while | flops 131074 | bytes 1048741 | solution.py:72
  170.7 4.3 collective-permute-start
  178.2 4.3 collective-permute-start
  186.3 4.3 collective-permute-start
  194.5 4.3 collective-permute-start
  203.2 4.3 collective-permute-start
  212.0 4.3 collective-permute-start
  220.7 4.3 collective-permute-start
  229.5 4.3 collective-permute-start
  238.2 4.3 collective-permute-start
  247.0 4.3 collective-permute-start
  255.7 4.3 collective-permute-start
  264.5 4.3 collective-permute-start
  273.2 4.3 collective-permute-start
  282.0 4.3 collective-permute-start
  290.7 4.3 collective-permute-start
  299.5 4.3 collective-permute-start
  308.2 4.3 collective-permute-start
  317.0 4.3 collective-permute-start
  325.7 4.3 collective-permute-start
  335.1 4.3 collective-permute-start
  344.7 4.3 collective-permute-start
  373.7 4.3 collective-permute-start
  393.0 4.3 collective-permute-start
  421.9 4.3 collective-permute-start
  450.9 4.3 collective-permute-start
  470.2 4.3 collective-permute-start
  479.8 4.3 collective-permute-start
  499.1 4.3 collective-permute-start
  528.1 4.3 collective-permute-start
  557.0 4.3 collective-permute-start
  576.3 4.3 collective-permute-start
  605.3 4.3 collective-permute-start
  634.2 4.3 collective-permute-start
  653.5 4.3 collective-permute-start
  663.1 4.3 collective-permute-start
  682.4 4.3 collective-permute-start
  711.4 4.3 collective-permute-start
  740.3 4.3 collective-permute-start
  750.0 54.8 %while.50 = (s32[]{:T(128)}, f32[160,1024]{1,0:T(8,128)S(1)}, f32[16,1024]{1,0:T(8,128)}, f32[16,1024]{1,0:T(8,128)S(1)}, f32[16,1024]{1,0:T(8,128)}, /*index=5*...) while((s32[]{:T(128)}, f32[160,1024]{1,0:T(8,128)S(1)}, ...), condition=%wide.region_8.0_spmd.clone.clone, body=%wide.region_7.0_spmd.clone.clone.sunk | while | flops 1482051 | bytes 1369463 | solution.py:85
  804.8 8.0 fusion.31
  812.8 57.5 %reduce-scatter.2.cloned.1.call-done = f32[160,1024]{1,0:T(8,128)} async-done(((f32[160,4096]{1,0:T(8,128)}), f32[160,1024]{1,0:T(8,128)}) %reduce-scatter.2.cloned.1.call-update) | async-done | bytes 655376 | tf_op jit(solution)/shard_map/reduce_scatter | solution.py:95
  (558 shorter events, 598.9 us)
Async XLA Ops:
  6.5 798.2 %all-gather.2.cloned.1.call-start = ((), (), s32[]{:S(2)}) async-start(), calls=%async_computation.1 | async-start | bytes 8519680 | tf_op jit(solution)/shard_map/all_gather | solution.py:92
  7.4 13.4 %collective-permute-start.2 = (bf16[6,3,1024]{2,0,1:T(8,128)(2,1)S(1)}, bf16[6,3,1024]{2,0,1:T(8,128)(2,1)S(1)}, u32[]{:S(2)}, u32[]{:S(2)}) collective-permute-start(bf16[6,3,1024]{2,0,1:T(8,128)(2,1)S(1)} %slice.76), channel_id=1, source_target_pairs={{0,4},{4,8},{8,12},{12,16},{16,20},{20,24},{24,28},{28,32},{32,36}... | collective-permute-start | bytes 110600 | tf_op jit(solution)/shard_map/ppermute | solution.py:10
  40.3 830.0 %reduce-scatter.2.cloned.1.call-start = ((), (), s32[]{:S(2)}) async-start(), calls=%async_computation.2 | async-start | bytes 3276800 | tf_op jit(solution)/shard_map/reduce_scatter | solution.py:95
  194.5 7.4 collective-permute-start
  325.7 8.0 collective-permute-start
  335.1 8.3 collective-permute-start
  344.7 8.3 collective-permute-start
  354.4 8.3 collective-permute-start
  364.0 8.3 collective-permute-start
  373.7 8.3 collective-permute-start
  383.3 8.3 collective-permute-start
  393.0 8.3 collective-permute-start
  402.6 8.3 collective-permute-start
  412.3 8.3 collective-permute-start
  421.9 8.3 collective-permute-start
  431.6 8.3 collective-permute-start
  441.2 8.3 collective-permute-start
  450.9 8.3 collective-permute-start
  460.5 8.3 collective-permute-start
  470.2 8.3 collective-permute-start
  479.8 8.3 collective-permute-start
  489.5 8.3 collective-permute-start
  499.1 8.3 collective-permute-start
  508.8 8.3 collective-permute-start
  518.4 8.3 collective-permute-start
  528.1 8.3 collective-permute-start
  537.7 8.3 collective-permute-start
  547.4 8.3 collective-permute-start
  557.0 8.3 collective-permute-start
  566.7 8.3 collective-permute-start
  576.3 8.3 collective-permute-start
  586.0 8.3 collective-permute-start
  595.6 8.3 collective-permute-start
  605.3 8.3 collective-permute-start
  614.9 8.3 collective-permute-start
  624.5 8.3 collective-permute-start
  634.2 8.3 collective-permute-start
  643.8 8.3 collective-permute-start
  653.5 8.3 collective-permute-start
  663.1 8.3 collective-permute-start
  672.8 8.3 collective-permute-start
  682.4 8.3 collective-permute-start
  692.1 8.3 collective-permute-start
  701.7 8.3 collective-permute-start
  711.4 8.3 collective-permute-start
  721.0 8.3 collective-permute-start
  730.7 8.3 collective-permute-start
  740.3 8.3 collective-permute-start
  (91 other events, 585.2 us)
Sparse Core Ops, SparseCore 0:
  40.5 85.2 all-gather.1
  812.9 57.3 reduce-scatter.1
where the time goes:
time: 887 us; the launch traced here: 879 us
  starting transfers between devices  508 us (57%)
  waiting for transfers between devices  139 us (16%)
  other arithmetic  127 us (14%)
  local copies, waits for them, and re-layouts  61.3 us (7%)
  matrix products  25.6 us (3%)
  between operations  13.7 us (2%)
    ppermute x128, starting transfers between devices, from_behind(): return lax.ppermute(block, axis, route)  508 us
    ppermute x128, waiting for transfers between devices, from_behind(): return lax.ppermute(block, axis, route)  81.8 us
    reduce_scatter x1, waiting for transfers between devices, body(): lax.psum_scatter(partial_out, 'tp', scatter_dimension=1, tiled=True)  57.5 us
    reduce_sum x16, other arithmetic, first_pass(): end_im = end_im.at[mode].set(jnp.sum(flipped * sink, 0))  44.8 us
    sub x16, other arithmetic, second_pass(): return inflow + are[None] * cos1 - aim[None] * sin1  40.9 us
    dynamic_slice x32, local copies, waits for them, and re-layouts, first_pass(): filt = filt + res_re[mode][None] * cosk - res_im[mode][None] * sink  24.6 us
    another operation x32, other arithmetic  20.2 us
  transfers between devices with their start and end apart: 130, of which 64 were waited for; matrix products, arithmetic and copies ran while one was open for 21% of the time, Pallas kernels for 0%

commit v1 on v0

v1 whole, which is shorter than its diff:
```python
import functools

import jax
import jax.numpy as jnp
from jax import lax
from jax.experimental import pallas as pl
from jax.experimental.pallas import tpu as pltpu
from jax.sharding import PartitionSpec as P

MESH = pl.DeviceIdType.MESH
SUB = 8
HALO = 128
XH = 8
GROUP = 4
F32 = jnp.float32
BF16 = jnp.bfloat16


def mixer_kernel(
    n,
    x_ref,
    staps_ref,
    mtaps_ref,
    rate_ref,
    angle_ref,
    res_ref,
    skip_ref,
    hid_ref,
    xf,
    gext,
    gsend,
    ghalo,
    tail,
    qs,
    med,
    loc,
    hid32,
    xr,
    xi,
    qr,
    qi,
    pr_s,
    pi_s,
    a1_s,
    a2_s,
    rr_s,
    ri_s,
    b1_s,
    p20r,
    p20i,
    p40r,
    p40i,
    p80r,
    p80i,
    p160r,
    p160i,
    mt_s,
    ebuf,
    rbuf,
    obuf,
    sbuf,
    halo_send,
    halo_recv,
    s1,
    r1,
    s2,
    r2,
):
    rows, width = hid_ref.shape
    span = rows // SUB
    modes = rate_ref.shape[0]
    groups = modes // GROUP
    tiles = width // 128
    total = groups * tiles
    stride = n // total
    me = lax.axis_index("ctx")
    nxt = lax.rem(me + 1, n)

    def lanes(l):
        return pl.ds(pl.multiple_of(l * 128, 128), 128)

    def fixed_row(ref, r, l):
        return jnp.broadcast_to(ref[pl.ds(r, 1), lanes(l)], (SUB, 128))

    def row(ref, r, l):
        return ref[l, pl.ds(r, SUB, stride=0), :]

    def put(ref, value):
        for t in range(tiles):
            ref[t] = value[:, t * 128 : (t + 1) * 128]

    barrier = pltpu.get_barrier_semaphore()

    def greet(r, c):
        pl.semaphore_signal(
            barrier, inc=1, device_id={"ctx": lax.rem(me + r, n)}, device_id_type=MESH
        )
        return c

    lax.fori_loop(1, n, greet, 0)

    for t in range(tiles):
        mt_s[t] = mtaps_ref[:, pl.ds(t * 128, 128)]

    for s in range(3):
        for t in range(tiles):
            xf[s * tiles + t, pl.ds(0, XH), :] = jnp.zeros((XH, 128), F32)

        def widen(i, c, s=s):
            at = pl.multiple_of(i * 16, 16)
            to = pl.multiple_of(XH + i * 16, 8)
            block = x_ref[s, pl.ds(at, 16), :].astype(F32)
            for t in range(tiles):
                xf[s * tiles + t, pl.ds(to, 16), :] = block[:, t * 128 : (t + 1) * 128]
            return c

        lax.fori_loop(0, rows // 16, widen, 0)

    def short(s, l, first, last):
        taps = [fixed_row(staps_ref, s * 8 + j, l) for j in range(7)]
        got = {}
        for d in range(first - 6, last):
            got[d] = xf[s * tiles + l, pl.ds(XH + d, SUB, stride=span), :]
        out = []
        for k in range(first, last):
            acc = taps[0] * got[k]
            for j in range(1, 7):
                acc = acc + taps[j] * got[k - j]
            out.append(acc)
        return out

    def gates(l, first, last):
        a = short(1, l, first, last)
        b = short(2, l, first, last)
        for k in range(first, last):
            gate = (a[k - first] * b[k - first]).astype(BF16).astype(F32)
            gext[l, pl.ds(HALO + k, SUB, stride=span), :] = gate

    def queries(l, first, last):
        q = short(0, l, first, last)
        for k in range(first, last):
            qs[pl.ds(k * SUB, SUB), lanes(l)] = q[k - first]

    def own_gates(l, c):
        gates(l, 0, span)
        return c

    lax.fori_loop(0, tiles, own_gates, 0)

    def narrow(i, c):
        at = pl.multiple_of(i * 16, 16)
        for t in range(tiles):
            gsend[pl.ds(at, 16), pl.ds(t * 128, 128)] = gext[t, pl.ds(rows + at, 16), :].astype(BF16)
        return c

    lax.fori_loop(0, HALO // 16, narrow, 0)

    pl.semaphore_wait(barrier, n - 1)

    send_tail = pltpu.make_async_remote_copy(
        src_ref=x_ref.at[:, pl.ds(rows - 16, 16), :],
        dst_ref=tail,
        send_sem=halo_send.at[0],
        recv_sem=halo_recv.at[0],
        device_id={"ctx": nxt},
        device_id_type=MESH,
    )
    send_gate = pltpu.make_async_remote_copy(
        src_ref=gsend,
        dst_ref=ghalo,
        send_sem=halo_send.at[1],
        recv_sem=halo_recv.at[1],
        device_id={"ctx": nxt},
        device_id_type=MESH,
    )
    send_tail.start()
    send_gate.start()

    rate = rate_ref[...]
    angle = angle_ref[...]
    mag = jnp.exp(-rate)
    pr = mag * jnp.cos(angle)
    pi = mag * jnp.sin(angle)
    amp = jnp.sqrt(1.0 - jnp.exp(-2.0 * rate))
    rr = res_ref[0] * amp
    ri = res_ref[1] * amp
    put(pr_s, pr)
    put(pi_s, pi)
    put(a1_s, 2.0 * pr)
    put(a2_s, -(pr * pr + pi * pi))
    put(rr_s, rr)
    put(ri_s, ri)
    put(b1_s, -(rr * pr + ri * pi))

    def square(z):
        return z[0] * z[0] - z[1] * z[1], 2.0 * z[0] * z[1]

    z4 = square(square((pr, pi)))
    z16 = square(square(z4))
    z20 = (z16[0] * z4[0] - z16[1] * z4[1], z16[0] * z4[1] + z16[1] * z4[0])
    z40 = square(z20)
    z80 = square(z40)
    z160 = square(z80)
    for (fr, fi), z in zip(
        ((p20r, p20i), (p40r, p40i), (p80r, p80i), (p160r, p160i)), (z20, z40, z80, z160)
    ):
        put(fr, z[0])
        put(fi, z[1])

    sub = lax.broadcasted_iota(jnp.int32, (SUB, 128), 0)
    bits = [lax.rem(sub, 2) == 1, lax.rem(sub // 2, 2) == 1, sub >= 4]
    past = [sub >= 1, sub >= 2, sub >= 4]

    def powers(m, c):
        def at(l, cc):
            zr = jnp.where(bits[0], row(p20r, m, l), 1.0)
            zi = jnp.where(bits[0], row(p20i, m, l), 0.0)
            for bit, (fr, fi) in zip(bits[1:], ((p40r, p40i), (p80r, p80i))):
                ar = jnp.where(bit, row(fr, m, l), 1.0)
                ai = jnp.where(bit, row(fi, m, l), 0.0)
                zr, zi = zr * ar - zi * ai, zr * ai + zi * ar
            to = pl.ds(pl.multiple_of(m * SUB, SUB), SUB)
            qr[to, lanes(l)] = zr
            qi[to, lanes(l)] = zi
            return cc

        return lax.fori_loop(0, tiles, at, c)

    lax.fori_loop(0, modes, powers, 0)

    send_tail.wait_recv()
    for s in range(3):
        rim = jnp.where(me > 0, tail[s].astype(F32)[8:], 0.0)
        for t in range(tiles):
            xf[s * tiles + t, pl.ds(0, XH), :] = rim[:, t * 128 : (t + 1) * 128]

    def rim_rows(l, c):
        gates(l, 0, 6)
        queries(l, 0, span)
        return c

    lax.fori_loop(0, tiles, rim_rows, 0)

    send_gate.wait_recv()

    def rim_gates(i, c):
        at = pl.ds(pl.multiple_of(i * 16, 16), 16)
        rim = jnp.where(me > 0, ghalo[at, :].astype(F32), 0.0)
        for t in range(tiles):
            gext[t, at, :] = rim[:, t * 128 : (t + 1) * 128]
        return c

    lax.fori_loop(0, HALO // 16, rim_gates, 0)

    def first_send(q, dest):
        return pltpu.make_async_remote_copy(
            src_ref=ebuf.at[q],
            dst_ref=rbuf.at[me],
            send_sem=s1,
            recv_sem=r1,
            device_id={"ctx": dest},
            device_id_type=MESH,
        )

    def tile(l, c):
        def taps8(jb, acc):
            base = HALO - jb * 8
            taps = [row(mt_s, jb * 8 + jj, l) for jj in range(8)]
            got = {
                d: gext[l, pl.ds(base + d, SUB, stride=span), :]
                for d in range(-7, span)
            }
            out = []
            for k in range(span):
                v = acc[k]
                for jj in range(8):
                    v = v + taps[jj] * got[k - jj]
                out.append(v)
            return tuple(out)

        zero = jnp.zeros((SUB, 128), F32)
        acc = lax.fori_loop(0, HALO // 8, taps8, (zero,) * span)
        for k in range(span):
            med[pl.ds(k * SUB, SUB), lanes(l)] = acc[k]

        def ends(g, cc):
            ms = [g * GROUP + i for i in range(GROUP)]
            a1 = [row(a1_s, m, l) for m in ms]
            a2 = [row(a2_s, m, l) for m in ms]
            w1 = [zero] * GROUP
            w2 = [zero] * GROUP
            for k in range(span):
                x = med[pl.ds(k * SUB, SUB), lanes(l)]
                w = [x + a1[i] * w1[i] + a2[i] * w2[i] for i in range(GROUP)]
                w2 = w1
                w1 = w
            q = l * groups + g
            for i, m in enumerate(ms):
                er = w1[i] - row(pr_s, m, l) * w2[i]
                ei = row(pi_s, m, l) * w2[i]
                for d, keep, (fr, fi) in zip(
                    (1, 2, 4), past, ((p20r, p20i), (p40r, p40i), (p80r, p80i))
                ):
                    br = jnp.where(keep, pltpu.roll(er, d, 0), 0.0)
                    bi = jnp.where(keep, pltpu.roll(ei, d, 0), 0.0)
                    ar = row(fr, m, l)
                    ai = row(fi, m, l)
                    er, ei = er + ar * br - ai * bi, ei + ar * bi + ai * br
                to = pl.ds(pl.multiple_of(m * SUB, SUB), SUB)
                xr[to, lanes(l)] = jnp.where(past[0], pltpu.roll(er, 1, 0), 0.0)
                xi[to, lanes(l)] = jnp.where(past[0], pltpu.roll(ei, 1, 0), 0.0)
                ebuf[q, pl.ds(i, 1), :] = er[SUB - 1 :, :]
                ebuf[q, pl.ds(GROUP + i, 1), :] = ei[SUB - 1 :, :]
            dest = q * stride

            @pl.when(dest != me)
            def _():
                first_send(q, dest).start()

            @pl.when(dest == me)
            def _():
                rbuf[me] = ebuf[q]

            return cc

        return lax.fori_loop(0, groups, ends, c)

    lax.fori_loop(0, tiles, tile, 0)

    def local(l, c):
        def part(g, acc):
            out = list(acc)
            ms = [g * GROUP + i for i in range(GROUP)]
            a1 = [row(a1_s, m, l) for m in ms]
            a2 = [row(a2_s, m, l) for m in ms]
            b0 = [row(rr_s, m, l) for m in ms]
            b1 = [row(b1_s, m, l) for m in ms]
            zero = jnp.zeros((SUB, 128), F32)
            w1 = [zero] * GROUP
            w2 = [zero] * GROUP
            for k in range(span):
                x = med[pl.ds(k * SUB, SUB), lanes(l)]
                w = [x + a1[i] * w1[i] + a2[i] * w2[i] for i in range(GROUP)]
                for i in range(GROUP):
                    out[k] = out[k] + (b0[i] * w[i] + b1[i] * w1[i])
                w2 = w1
                w1 = w
            return tuple(out)

        skip = fixed_row(skip_ref, 0, l)
        acc = tuple(skip * med[pl.ds(k * SUB, SUB), lanes(l)] for k in range(span))
        acc = lax.fori_loop(0, groups, part, acc)
        for k in range(span):
            loc[pl.ds(k * SUB, SUB), lanes(l)] = acc[k]
        return c

    lax.fori_loop(0, tiles, local, 0)

    mine = me // stride
    scans = lax.rem(me, stride) == 0

    def reply(i):
        return pltpu.make_async_remote_copy(
            src_ref=obuf.at[i],
            dst_ref=sbuf.at[mine],
            send_sem=s2,
            recv_sem=r2,
            device_id={"ctx": i},
            device_id_type=MESH,
        )

    def await_tiles(ref, count, sem):
        part = ref.at[pl.ds(0, count)]
        pltpu.make_async_copy(part, part, sem).wait()

    @pl.when(scans)
    def _():
        await_tiles(rbuf, n - 1, r1)
        l = mine // groups
        g = lax.rem(mine, groups)
        dr = jnp.zeros((SUB, 128), F32)
        di = jnp.zeros((SUB, 128), F32)
        for i in range(GROUP):
            here = lax.rem(sub, GROUP) == i
            dr = jnp.where(here, row(p160r, g * GROUP + i, l), dr)
            di = jnp.where(here, row(p160i, g * GROUP + i, l), di)
        di = jnp.where(sub < GROUP, -di, di)

        def block(i, st):
            obuf[i] = st
            return dr * st + di * pltpu.roll(st, GROUP, 0) + rbuf[i]

        lax.fori_loop(0, n, block, jnp.zeros((SUB, 128), F32), unroll=8)

        def answer(r, c):
            reply(lax.rem(me + r, n)).start()
            return c

        lax.fori_loop(1, n, answer, 0)
        sbuf[mine] = obuf[me]
        await_tiles(sbuf, total - 1, r2)

    @pl.when(jnp.logical_not(scans))
    def _():
        await_tiles(sbuf, total, r2)

    def finish(l, c):
        def part(g, acc):
            out = list(acc)
            q = l * groups + g
            for i in range(GROUP):
                m = g * GROUP + i
                inr = jnp.broadcast_to(sbuf[q, pl.ds(i, 1), :], (SUB, 128))
                ini = jnp.broadcast_to(sbuf[q, pl.ds(GROUP + i, 1), :], (SUB, 128))
                at = pl.ds(pl.multiple_of(m * SUB, SUB), SUB)
                zr = qr[at, lanes(l)]
                zi = qi[at, lanes(l)]
                sr = xr[at, lanes(l)] + zr * inr - zi * ini
                si = xi[at, lanes(l)] + zr * ini + zi * inr
                rr = row(rr_s, m, l)
                ri = row(ri_s, m, l)
                ar = rr * sr - ri * si
                ai = rr * si + ri * sr
                u2 = ar
                u1 = ar * row(pr_s, m, l) - ai * row(pi_s, m, l)
                a1 = row(a1_s, m, l)
                a2 = row(a2_s, m, l)
                for k in range(span):
                    out[k] = out[k] + u1
                    u1, u2 = a1 * u1 + a2 * u2, u1
            return tuple(out)

        acc = tuple(loc[pl.ds(k * SUB, SUB), lanes(l)] for k in range(span))
        acc = lax.fori_loop(0, groups, part, acc)
        for k in range(span):
            hid = qs[pl.ds(k * SUB, SUB), lanes(l)] * acc[k]
            hid32[l, pl.ds(k, SUB, stride=span), :] = hid
        return c

    lax.fori_loop(0, tiles, finish, 0)

    def pack(i, c):
        at = pl.ds(pl.multiple_of(i * 16, 16), 16)
        for t in range(tiles):
            hid_ref[at, pl.ds(t * 128, 128)] = hid32[t, at, :].astype(BF16)
        return c

    lax.fori_loop(0, rows // 16, pack, 0)

    send_tail.wait_send()
    send_gate.wait_send()

    @pl.when(scans)
    def _():
        await_tiles(ebuf, total - 1, s1)
        await_tiles(obuf, n - 1, s2)

    @pl.when(jnp.logical_not(scans))
    def _():
        await_tiles(ebuf, total, s1)


def project_kernel(n, h_ref, w_ref, out_ref, sent, got, send_sem, recv_sem):
    rows, width = out_ref.shape
    me = lax.axis_index("tp")
    barrier = pltpu.get_barrier_semaphore()
    for r in range(1, n):
        pl.semaphore_signal(
            barrier, inc=1, device_id={"tp": lax.rem(me + r, n)}, device_id_type=MESH
        )

    def chunk(owner):
        cols = pl.ds(pl.multiple_of(owner * width, 128), width)
        return jnp.dot(h_ref[...], w_ref[:, cols], preferred_element_type=F32)

    copies = []
    for r in (2, 1, 3)[: n - 1] if n == 4 else range(1, n):
        to = lax.rem(me + r, n)
        sent[r - 1] = chunk(to).astype(BF16)
        if not copies:
            pl.semaphore_wait(barrier, n - 1)
        copy = pltpu.make_async_remote_copy(
            src_ref=sent.at[r - 1],
            dst_ref=got.at[r - 1],
            send_sem=send_sem.at[r - 1],
            recv_sem=recv_sem.at[r - 1],
            device_id={"tp": to},
            device_id_type=MESH,
        )
        copy.start()
        copies.append(copy)
    acc = chunk(me)
    for copy in copies:
        copy.wait_recv()
    for r in range(n - 1):
        acc = acc + got[r].astype(F32)
    out_ref[...] = acc.astype(BF16)
    for copy in copies:
        copy.wait_send()


def vmem(shape, dtype=F32):
    return pltpu.VMEM(shape, dtype)


def body(n_ctx, n_tp, streams, short_taps, mix_taps, pole_rate, pole_angle, residue, skip, out_weight):
    rows, three, width = streams.shape
    modes = pole_rate.shape[0]
    x = streams.transpose(1, 0, 2)
    staps = jnp.pad(short_taps.transpose(1, 0, 2), ((0, 0), (0, 1), (0, 0))).reshape(24, width)
    tiles = width // 128
    total = (modes // GROUP) * tiles
    coef = [vmem((tiles, modes, 128))] * 15
    vm = pl.BlockSpec(memory_space=pltpu.VMEM)
    weight = lax.all_gather(out_weight, "ctx", axis=1, tiled=True)
    hidden = pl.pallas_call(
        functools.partial(mixer_kernel, n_ctx),
        out_shape=jax.ShapeDtypeStruct((rows, width), BF16),
        in_specs=[vm] * 7,
        out_specs=vm,
        scratch_shapes=[
            vmem((3 * tiles, XH + rows, 128)),
            vmem((tiles, HALO + rows, 128)),
            vmem((HALO, width), BF16),
            vmem((HALO, width), BF16),
            vmem((3, 16, width), BF16),
            vmem((rows, width)),
            vmem((rows, width)),
            vmem((rows, width)),
            vmem((tiles, rows, 128)),
            vmem((modes * SUB, width)),
            vmem((modes * SUB, width)),
            vmem((modes * SUB, width)),
            vmem((modes * SUB, width)),
            *coef,
            vmem((tiles, HALO, 128)),
            vmem((total, 8, 128)),
            vmem((n_ctx, 8, 128)),
            vmem((n_ctx, 8, 128)),
            vmem((total, 8, 128)),
            pltpu.SemaphoreType.DMA((2,)),
            pltpu.SemaphoreType.DMA((2,)),
            pltpu.SemaphoreType.DMA,
            pltpu.SemaphoreType.DMA,
            pltpu.SemaphoreType.DMA,
            pltpu.SemaphoreType.DMA,
        ],
        compiler_params=pltpu.CompilerParams(collective_id=0, has_side_effects=True),
        name="mixer",
    )(x, staps, mix_taps, pole_rate, pole_angle, residue, skip[None])
    cols = weight.shape[1] // n_tp
    return pl.pallas_call(
        functools.partial(project_kernel, n_tp),
        out_shape=jax.ShapeDtypeStruct((rows, cols), BF16),
        in_specs=[vm] * 2,
        out_specs=vm,
        scratch_shapes=[
            vmem((n_tp - 1, rows, cols), BF16),
            vmem((n_tp - 1, rows, cols), BF16),
            pltpu.SemaphoreType.DMA((n_tp - 1,)),
            pltpu.SemaphoreType.DMA((n_tp - 1,)),
        ],
        compiler_params=pltpu.CompilerParams(collective_id=1, has_side_effects=True),
        name="project",
    )(hidden, weight)


def solution(mesh):
    return jax.shard_map(
        functools.partial(body, mesh.shape["ctx"], mesh.shape["tp"]),
        mesh=mesh,
        in_specs=(
            P("ctx", None, "tp"),
            P(None, None, "tp"),
            P(None, "tp"),
            P(None, "tp"),
            P(None, "tp"),
            P(None, None, "tp"),
            P("tp"),
            P("tp", "ctx"),
        ),
        out_specs=P("ctx", "tp"),
        check_vma=False,
    )
```

time: 887 us -> 142 us (0.16)
  starting transfers between devices: 508 us -> 0.01 us
  other arithmetic: 127 us -> 0 us
  waiting for transfers between devices: 139 us -> 44.8 us
  Pallas kernels: 0 us -> 68.4 us
  local copies, waits for them, and re-layouts: 61.3 us -> 14.6 us
  matrix products: 25.6 us -> 0 us
    ppermute x128 -> x0, starting transfers between devices: 508 us -> none  [from_behind(): return lax.ppermute(block, axis, route)]
    ppermute x128 -> x0, waiting for transfers between devices: 81.8 us -> none  [from_behind(): return lax.ppermute(block, axis, route)]
    pallas_call x0 -> x2, Pallas kernels: none -> 68.4 us  [the longest x1 44.6 us: body(): pl.pallas_call(functools.partial(mixer_kernel, n_ctx), out_shape=jax.Shap...]
    reduce_scatter x1 -> x0, waiting for transfers between devices: 57.5 us -> none  [body(): lax.psum_scatter(partial_out, 'tp', scatter_dimension=1, tiled=True)]
    sub x32 -> x0, other arithmetic: 53.8 us -> none  [the longest x16 40.9 us: second_pass(): return inflow + are[None] * cos1 - aim[None] * sin1]
    reduce_sum x16 -> x0, other arithmetic: 44.8 us -> none  [first_pass(): end_im = end_im.at[mode].set(jnp.sum(flipped * sink, 0))]
    all_gather x1, waiting for transfers between devices: 0.02 us -> 44.1 us  [body(): weight = lax.all_gather(out_weight, 'ctx', axis=1, tiled=True)]
    dynamic_slice x64 -> x0, local copies, waits for them, and re-layouts: 25 us -> none  [the longest x32 24.6 us: first_pass(): filt = filt + res_re[mode][None] * cosk - res_im[mode][None] * sink]
  transfers between devices with their start and end apart: 130 -> 1, of which waited for: 64 -> 1; matrix products, arithmetic and copies ran while one was open for 21% -> 1% of each run, Pallas kernels for 0% -> 32%
where the time goes in v1:
time: 142 us; the launch traced here: 141 us
  Pallas kernels  68.4 us (48%)
  waiting for transfers between devices  44.8 us (32%)
  local copies, waits for them, and re-layouts  14.6 us (10%)
  between operations  13.4 us (9%)
    pallas_call x1, Pallas kernels, body(): pl.pallas_call(functools.partial(mixer_kernel, n_ctx), out_shape=jax.Shap...  44.6 us
    all_gather x1, waiting for transfers between devices, body(): weight = lax.all_gather(out_weight, 'ctx', axis=1, tiled=True)  44.1 us
    pallas_call x1, Pallas kernels, body(): pl.pallas_call(functools.partial(project_kernel, n_tp), out_shape=jax.Sha...  23.8 us
    all_gather x1, local copies, waits for them, and re-layouts, body(): weight = lax.all_gather(out_weight, 'ctx', axis=1, tiled=True)  11.4 us
  transfers between devices with their start and end apart: 1, of which 1 were waited for; matrix products, arithmetic and copies ran while one was open for 1% of the time, Pallas kernels for 32%

profile of v1, /device:TPU:1, one launch (start us, length us, event | category | flops | bytes accessed | tf_op | source)
XLA Modules:
  0.0 141.2 jit_solution(1782432805668557609)
XLA Ops:
  6.5 0.0 all-gather.2.cloned.1.call-start
  6.5 0.7 all-gather.2.cloned.1.call-update
  7.3 1.5 %pad_bitcast_fusion.staps_ref = f32[24,1024]{1,0:T(8,128)} fusion(f32[3,7,1024]{2,1,0:T(8,128)} %bitcast.6), kind=kLoop, calls=%fused_computation | loop fusion | bytes 184320 | tf_op jit(solution)/shard_map/reshape | solution.py:510
  8.8 44.6 %mixer.1.h_ref = bf16[160,1024]{1,0:T(8,128)(2,1)} custom-call(bf16[3,160,1024]{2,1,0:T(8,128)(2,1)} %bitcast.5, f32[24,1024]{1,0:T(8,128)} %pad_bitcast_fusion.staps_ref, f32[128,1024]{1,0:T(8,128)} %mtaps_ref.1, f32[16,1024]{1,0:T(8,128)} %rate_ref.1, f32[16,1024]{1,0:T(8,128)} %angle_ref.1, f32[2,16,1024]{2,1,0:T(8,128)} %res_ref.1, f32[1,1024]{1,0:T(1,128)} %bitcast.7), custom_call_target="tpu_custom_call" | custom-call | tf_op jit(solution)/shard_map/mixer/pallas_call | solution.py:516
  53.4 44.1 %all-gather.2.cloned.1.call-done = bf16[1024,4096]{0,1:T(8,128)(2,1)} async-done(((bf16[1024,64]{0,1:T(8,128)(2,1)}), bf16[1024,4096]{0,1:T(8,128)(2,1)}) %all-gather.2.cloned.1.call-update) | async-done | bytes 8388624 | tf_op jit(solution)/shard_map/all_gather | solution.py:515
  97.5 11.4 %copy.10.w_ref = bf16[1024,4096]{1,0:T(8,128)(2,1)} copy(bf16[1024,4096]{0,1:T(8,128)(2,1)} %all-gather.2.cloned.1.call-done) | data formatting | bytes 16777216 | tf_op jit(solution)/shard_map/all_gather | solution.py:515
  108.9 23.8 %project.1 = bf16[160,1024]{1,0:T(8,128)(2,1)} custom-call(bf16[160,1024]{1,0:T(8,128)(2,1)} %mixer.1.h_ref, bf16[1024,4096]{1,0:T(8,128)(2,1)} %copy.10.w_ref), custom_call_target="tpu_custom_call" | custom-call | tf_op jit(solution)/shard_map/project/pallas_call | solution.py:552
  132.7 1.7 %copy.12 = bf16[160,1024]{1,0:T(8,128)(2,1)} copy(bf16[160,1024]{1,0:T(8,128)(2,1)} %project.1) | data formatting | bytes 655360
Async XLA Ops:
  6.5 91.0 %all-gather.2.cloned.1.call-start = ((), (), s32[]{:S(2)}) async-start(), calls=%async_computation | async-start | bytes 8519680 | tf_op jit(solution)/shard_map/all_gather | solution.py:515
Sparse Core Ops, SparseCore 0:
  10.1 87.3 all-gather.1

commit v2 on v1

--- a/solution.py
+++ b/solution.py
@@ -16,8 +16,9 @@
 BF16 = jnp.bfloat16
 
 
-def mixer_kernel(
+def block_kernel(
     n,
+    n_tp,
     x_ref,
     staps_ref,
     mtaps_ref,
@@ -25,7 +26,8 @@
     angle_ref,
     res_ref,
     skip_ref,
-    hid_ref,
+    w_ref,
+    out_ref,
     xf,
     gext,
     gsend,
@@ -65,8 +67,32 @@
     r1,
     s2,
     r2,
+    wt,
+    h2,
+    own_sem,
+    a1s,
+    a1r,
+    ps,
+    pr_,
+    ms,
+    mr,
+    h_send,
+    h_recv,
+    part,
+    snd,
+    rcv,
+    rcvp,
+    fin,
+    y_send,
+    y_recv,
+    c_send,
+    c_recv,
 ):
-    rows, width = hid_ref.shape
+    _, rows, width = x_ref.shape
+    n_x = n_tp
+    n_z = n // (2 * n_x)
+    wide = w_ref.shape[0]
+    tp = lax.axis_index("tp")
     span = rows // SUB
     modes = rate_ref.shape[0]
     groups = modes // GROUP
@@ -75,6 +101,79 @@
     stride = n // total
     me = lax.axis_index("ctx")
     nxt = lax.rem(me + 1, n)
+    core = lax.rem(me, 2)
+    z = lax.rem(me // 2, n_z)
+    x = me // (2 * n_z)
+    other = me + 1 - 2 * core
+
+    def at_x(dx):
+        return lax.rem(x + dx + n_x, n_x)
+
+    def at_z(dz):
+        return lax.rem(z + dz + n_z, n_z)
+
+    def device(xx, zz):
+        return {"ctx": (xx * n_z + zz) * 2 + core}
+
+    order = [0]
+    for d in range(1, n_z // 2 + 1):
+        order += [d] if 2 * d == n_z else [d, -d]
+
+    own_block = pltpu.make_async_copy(w_ref, wt.at[x * n_z + z], own_sem)
+    own_block.start()
+
+    def along_z(dz):
+        return pltpu.make_async_remote_copy(
+            src_ref=w_ref,
+            dst_ref=wt.at[x * n_z + z],
+            send_sem=a1s.at[dz % n_z],
+            recv_sem=a1r.at[(-dz) % n_z],
+            device_id=device(x, at_z(dz)),
+            device_id_type=MESH,
+        )
+
+    def from_z(dz):
+        block = wt.at[x * n_z + at_z(dz)]
+        return pltpu.make_async_copy(block, block, a1r.at[dz % n_z])
+
+    def along_x(step, hop, p):
+        send, recv = (ps, pr_) if step > 0 else (ms, mr)
+        block = wt.at[at_x(-step * hop) * n_z + at_z(order[p])]
+        return pltpu.make_async_remote_copy(
+            src_ref=block,
+            dst_ref=block,
+            send_sem=send.at[hop * n_z + p],
+            recv_sem=recv.at[hop * n_z + p],
+            device_id=device(at_x(step), z),
+            device_id_type=MESH,
+        )
+
+    def from_x(step, hop, p):
+        recv = pr_ if step > 0 else mr
+        block = wt.at[at_x(-step * (hop + 1)) * n_z + at_z(order[p])]
+        return pltpu.make_async_copy(block, block, recv.at[hop * n_z + p])
+
+    steps = (1, -1) if n_x > 2 else (1,)
+    passed = {1: [], -1: []}
+    if n_x == 4:
+        passed = {1: [p for p in range(n_z) if p % 2 == 0], -1: [p for p in range(n_z) if p % 2 == 1]}
+    started = []
+
+    def give(*ps_):
+        for p in ps_:
+            if p < n_z:
+                if p:
+                    from_z(order[p]).wait()
+                for step in steps:
+                    along_x(step, 0, p).start()
+                    started.append((step, 0, p))
+
+    def hand_on(step, *ps_):
+        for p in ps_:
+            if p in passed[step]:
+                from_x(step, 0, p).wait()
+                along_x(step, 1, p).start()
+                started.append((step, 1, p))
 
     def lanes(l):
         return pl.ds(pl.multiple_of(l * 128, 128), 128)
@@ -98,6 +197,14 @@
         return c
 
     lax.fori_loop(1, n, greet, 0)
+    for r in range(1, n_tp):
+        for who in (me, other):
+            pl.semaphore_signal(
+                barrier,
+                inc=1,
+                device_id={"ctx": who, "tp": lax.rem(tp + r, n_tp)},
+                device_id_type=MESH,
+            )
 
     for t in range(tiles):
         mt_s[t] = mtaps_ref[:, pl.ds(t * 128, 128)]
@@ -117,7 +224,7 @@
         lax.fori_loop(0, rows // 16, widen, 0)
 
     def short(s, l, first, last):
-        taps = [fixed_row(staps_ref, s * 8 + j, l) for j in range(7)]
+        taps = [jnp.broadcast_to(staps_ref[s, pl.ds(j, 1), lanes(l)], (SUB, 128)) for j in range(7)]
         got = {}
         for d in range(first - 6, last):
             got[d] = xf[s * tiles + l, pl.ds(XH + d, SUB, stride=span), :]
@@ -155,7 +262,7 @@
 
     lax.fori_loop(0, HALO // 16, narrow, 0)
 
-    pl.semaphore_wait(barrier, n - 1)
+    pl.semaphore_wait(barrier, n - 1 + 2 * (n_tp - 1))
 
     send_tail = pltpu.make_async_remote_copy(
         src_ref=x_ref.at[:, pl.ds(rows - 16, 16), :],
@@ -201,11 +308,11 @@
     z40 = square(z20)
     z80 = square(z40)
     z160 = square(z80)
-    for (fr, fi), z in zip(
+    for (fr, fi), power in zip(
         ((p20r, p20i), (p40r, p40i), (p80r, p80i), (p160r, p160i)), (z20, z40, z80, z160)
     ):
-        put(fr, z[0])
-        put(fi, z[1])
+        put(fr, power[0])
+        put(fi, power[1])
 
     sub = lax.broadcasted_iota(jnp.int32, (SUB, 128), 0)
     bits = [lax.rem(sub, 2) == 1, lax.rem(sub // 2, 2) == 1, sub >= 4]
@@ -251,6 +358,11 @@
         return c
 
     lax.fori_loop(0, HALO // 16, rim_gates, 0)
+
+    own_block.wait()
+    give(0)
+    for dz in order[1:]:
+        along_z(dz).start()
 
     def first_send(q, dest):
         return pltpu.make_async_remote_copy(
@@ -327,6 +439,9 @@
 
     lax.fori_loop(0, tiles, tile, 0)
 
+    give(1, 2)
+    hand_on(1, 0)
+
     def local(l, c):
         def part(g, acc):
             out = list(acc)
@@ -356,6 +471,10 @@
 
     lax.fori_loop(0, tiles, local, 0)
 
+    give(3, 4)
+    hand_on(1, 2)
+    hand_on(-1, 1)
+
     mine = me // stride
     scans = lax.rem(me, stride) == 0
 
@@ -398,6 +517,13 @@
 
         lax.fori_loop(1, n, answer, 0)
         sbuf[mine] = obuf[me]
+
+    give(5, 6)
+    hand_on(1, 4)
+    hand_on(-1, 3)
+
+    @pl.when(scans)
+    def _():
         await_tiles(sbuf, total - 1, r2)
 
     @pl.when(jnp.logical_not(scans))
@@ -435,17 +561,132 @@
         for k in range(span):
             hid = qs[pl.ds(k * SUB, SUB), lanes(l)] * acc[k]
             hid32[l, pl.ds(k, SUB, stride=span), :] = hid
+        h2[core, :, lanes(l)] = hid32[l].astype(BF16)
+        send_hidden(l).start()
         return c
 
+    def send_hidden(l):
+        return pltpu.make_async_remote_copy(
+            src_ref=h2.at[core, :, lanes(l)],
+            dst_ref=h2.at[core, :, lanes(l)],
+            send_sem=h_send,
+            recv_sem=h_recv,
+            device_id={"ctx": other},
+            device_id_type=MESH,
+        )
+
     lax.fori_loop(0, tiles, finish, 0)
 
-    def pack(i, c):
+    give(*range(7, n_z))
+    hand_on(-1, 5)
+    hand_on(1, 6)
+    hand_on(-1, 7)
+    pltpu.make_async_copy(h2.at[1 - core], h2.at[1 - core], h_recv).wait()
+
+    half = n_z * wide
+
+    def to_y(k, to, r):
+        return [
+            pltpu.make_async_remote_copy(
+                src_ref=snd.at[k, cc],
+                dst_ref=rcv.at[r - 1, core],
+                send_sem=y_send.at[k, cc],
+                recv_sem=y_recv.at[r - 1, core],
+                device_id={"ctx": me - core + cc, "tp": to},
+                device_id_type=MESH,
+            )
+            for cc in range(2)
+        ]
+
+    to_core = pltpu.make_async_remote_copy(
+        src_ref=part.at[1 - core],
+        dst_ref=rcvp,
+        send_sem=c_send,
+        recv_sem=c_recv,
+        device_id={"ctx": other},
+        device_id_type=MESH,
+    )
+    turns = [0, 1, -1, 2][:n_x] if n_x == 4 else list(range(n_x))
+    for k, dx in enumerate(turns):
+        if dx == 1 and n_x == 4:
+            for p in range(n_z):
+                if p not in passed[-1]:
+                    from_x(-1, 0, p).wait()
+        elif dx == -1 or dx == 1:
+            for p in range(n_z):
+                if p not in passed[1]:
+                    from_x(1, 0, p).wait()
+        elif dx == 2:
+            for step in steps:
+                for p in passed[step]:
+                    from_x(step, 1, p).wait()
+        to = at_x(dx)
+        r = lax.rem(to - tp + n_tp, n_tp)
+        w = wt[pl.ds(to * n_z, n_z)].reshape(half, width)
+        for cc in range(2):
+            got = lax.dot_general(
+                h2[cc], w, (((1,), (1,)), ((), ())), preferred_element_type=F32
+            )
+
+            @pl.when(r == 0)
+            def _(got=got, cc=cc):
+                part[cc] = got
+
+            @pl.when(r != 0)
+            def _(got=got, cc=cc, k=k):
+                snd[k, cc] = got.astype(BF16)
+
+        @pl.when(r == 0)
+        def _():
+            to_core.start()
+
+        @pl.when(r != 0)
+        def _(k=k, to=to, r=r):
+            for copy in to_y(k, to, r):
+                copy.start()
+
+    def got_from(r, cc):
+        block = rcv.at[r - 1, cc]
+        pltpu.make_async_copy(block, block, y_recv.at[r - 1, cc]).wait()
+
+    to_core.wait_recv()
+    for r in range(1, n_tp):
+        for cc in range(2):
+            got_from(r, cc)
+
+    def add(i, c):
         at = pl.ds(pl.multiple_of(i * 16, 16), 16)
-        for t in range(tiles):
-            hid_ref[at, pl.ds(t * 128, 128)] = hid32[t, at, :].astype(BF16)
+        mine_sum = part[core, at, :]
+        other_sum = rcvp[at, :]
+        for r in range(1, n_tp):
+            mine_sum = mine_sum + rcv[r - 1, core, at, :].astype(F32)
+            other_sum = other_sum + rcv[r - 1, 1 - core, at, :].astype(F32)
+        fin[core, at, :] = mine_sum
+        fin[1 - core, at, :] = other_sum
+        low = lax.broadcasted_iota(jnp.int32, (16, 128), 1) < wide
+        for t in range(half // 128):
+            a = fin[0, at, pl.ds(t * 128, 128)]
+            b = fin[1, at, pl.ds(t * 128, 128)]
+            out_ref[at, pl.ds(t * 256, 128)] = jnp.where(low, a, pltpu.roll(b, wide, 1)).astype(BF16)
+            out_ref[at, pl.ds(t * 256 + 128, 128)] = jnp.where(low, pltpu.roll(a, wide, 1), b).astype(BF16)
         return c
 
-    lax.fori_loop(0, rows // 16, pack, 0)
+    lax.fori_loop(0, rows // 16, add, 0)
+
+    for dz in order[1:]:
+        along_z(dz).wait_send()
+    for what in started:
+        along_x(*what).wait_send()
+    pltpu.make_async_copy(h2.at[core], h2.at[core], h_send).wait()
+    to_core.wait_send()
+    for k, dx in enumerate(turns):
+        to = at_x(dx)
+        r = lax.rem(to - tp + n_tp, n_tp)
+
+        @pl.when(r != 0)
+        def _(k=k, to=to, r=r):
+            for copy in to_y(k, to, r):
+                copy.wait_send()
 
     send_tail.wait_send()
     send_gate.wait_send()
@@ -460,45 +701,6 @@
         await_tiles(ebuf, total, s1)
 
 
-def project_kernel(n, h_ref, w_ref, out_ref, sent, got, send_sem, recv_sem):
-    rows, width = out_ref.shape
-    me = lax.axis_index("tp")
-    barrier = pltpu.get_barrier_semaphore()
-    for r in range(1, n):
-        pl.semaphore_signal(
-            barrier, inc=1, device_id={"tp": lax.rem(me + r, n)}, device_id_type=MESH
-        )
-
-    def chunk(owner):
-        cols = pl.ds(pl.multiple_of(owner * width, 128), width)
-        return jnp.dot(h_ref[...], w_ref[:, cols], preferred_element_type=F32)
-
-    copies = []
-    for r in (2, 1, 3)[: n - 1] if n == 4 else range(1, n):
-        to = lax.rem(me + r, n)
-        sent[r - 1] = chunk(to).astype(BF16)
-        if not copies:
-            pl.semaphore_wait(barrier, n - 1)
-        copy = pltpu.make_async_remote_copy(
-            src_ref=sent.at[r - 1],
-            dst_ref=got.at[r - 1],
-            send_sem=send_sem.at[r - 1],
-            recv_sem=recv_sem.at[r - 1],
-            device_id={"tp": to},
-            device_id_type=MESH,
-        )
-        copy.start()
-        copies.append(copy)
-    acc = chunk(me)
-    for copy in copies:
-        copy.wait_recv()
-    for r in range(n - 1):
-        acc = acc + got[r].astype(F32)
-    out_ref[...] = acc.astype(BF16)
-    for copy in copies:
-        copy.wait_send()
-
-
 def vmem(shape, dtype=F32):
     return pltpu.VMEM(shape, dtype)
 
@@ -506,17 +708,17 @@
 def body(n_ctx, n_tp, streams, short_taps, mix_taps, pole_rate, pole_angle, residue, skip, out_weight):
     rows, three, width = streams.shape
     modes = pole_rate.shape[0]
-    x = streams.transpose(1, 0, 2)
-    staps = jnp.pad(short_taps.transpose(1, 0, 2), ((0, 0), (0, 1), (0, 0))).reshape(24, width)
     tiles = width // 128
     total = (modes // GROUP) * tiles
+    cols = out_weight.shape[1]
+    half = n_ctx // (2 * n_tp) * cols
     coef = [vmem((tiles, modes, 128))] * 15
     vm = pl.BlockSpec(memory_space=pltpu.VMEM)
-    weight = lax.all_gather(out_weight, "ctx", axis=1, tiled=True)
-    hidden = pl.pallas_call(
-        functools.partial(mixer_kernel, n_ctx),
-        out_shape=jax.ShapeDtypeStruct((rows, width), BF16),
-        in_specs=[vm] * 7,
+    hbm = pl.BlockSpec(memory_space=pl.ANY)
+    return pl.pallas_call(
+        functools.partial(block_kernel, n_ctx, n_tp),
+        out_shape=jax.ShapeDtypeStruct((rows, 2 * half), BF16),
+        in_specs=[vm] * 7 + [hbm],
         out_specs=vm,
         scratch_shapes=[
             vmem((3 * tiles, XH + rows, 128)),
@@ -544,25 +746,34 @@
             pltpu.SemaphoreType.DMA,
             pltpu.SemaphoreType.DMA,
             pltpu.SemaphoreType.DMA,
+            vmem((n_ctx // 2, cols, width), BF16),
+            vmem((2, rows, width), BF16),
+            pltpu.SemaphoreType.DMA,
+            *[pltpu.SemaphoreType.DMA((n_ctx // n_tp,))] * 6,
+            pltpu.SemaphoreType.DMA,
+            pltpu.SemaphoreType.DMA,
+            vmem((2, rows, half)),
+            vmem((n_tp, 2, rows, half), BF16),
+            vmem((n_tp - 1, 2, rows, half), BF16),
+            vmem((rows, half)),
+            vmem((2, rows, half)),
+            pltpu.SemaphoreType.DMA((n_tp, 2)),
+            pltpu.SemaphoreType.DMA((n_tp - 1, 2)),
+            pltpu.SemaphoreType.DMA,
+            pltpu.SemaphoreType.DMA,
         ],
         compiler_params=pltpu.CompilerParams(collective_id=0, has_side_effects=True),
-        name="mixer",
-    )(x, staps, mix_taps, pole_rate, pole_angle, residue, skip[None])
-    cols = weight.shape[1] // n_tp
-    return pl.pallas_call(
-        functools.partial(project_kernel, n_tp),
-        out_shape=jax.ShapeDtypeStruct((rows, cols), BF16),
-        in_specs=[vm] * 2,
-        out_specs=vm,
-        scratch_shapes=[
-            vmem((n_tp - 1, rows, cols), BF16),
-            vmem((n_tp - 1, rows, cols), BF16),
-            pltpu.SemaphoreType.DMA((n_tp - 1,)),
-            pltpu.SemaphoreType.DMA((n_tp - 1,)),
-        ],
-        compiler_params=pltpu.CompilerParams(collective_id=1, has_side_effects=True),
-        name="project",
-    )(hidden, weight)
+        name="hyena_block",
+    )(
+        streams.transpose(1, 0, 2),
+        short_taps.transpose(1, 0, 2),
+        mix_taps,
+        pole_rate,
+        pole_angle,
+        residue,
+        skip[None],
+        out_weight.T,
+    )
 
 
 def solution(mesh):

time: 142 us -> 86.8 us (0.61)
  the two profiles are of different devices: /device:TPU:1 before, /device:TPU:5 now
where the time goes in v2:
time: 86.8 us; the launch traced here: 86.7 us
  Pallas kernels  85 us (98%)
  local copies, waits for them, and re-layouts  1.72 us (2%)
    pallas_call x1, Pallas kernels, body(): pl.pallas_call(functools.partial(block_kernel, n_ctx, n_tp), out_shape=ja...  85 us

profile of v2, /device:TPU:5, one launch (start us, length us, event | category | flops | bytes accessed | tf_op | source)
XLA Modules:
  0.0 86.7 jit_solution(17347006029396765459)
XLA Ops:
  0.0 85.0 %hyena_block.1 = bf16[160,1024]{1,0:T(8,128)(2,1)} custom-call(bf16[3,160,1024]{2,1,0:T(8,128)(2,1)} %bitcast.4, f32[3,7,1024]{2,1,0:T(8,128)} %bitcast.6, f32[128,1024]{1,0:T(8,128)} %mtaps_ref.1, f32[16,1024]{1,0:T(8,128)} %rate_ref.1, f32[16,1024]{1,0:T(8,128)} %angle_ref.1, f32[2,16,1024]{2,1,0:T(8,128)} %res_ref.1, f32[1,1024]{1,0:T(1,128)} %bitcast.7, ...), custom_call_target="tpu_custom_call" | custom-call | tf_op jit(solution)/shard_map/hyena_block/pallas_call | solution.py:718
  85.0 1.7 %copy.10 = bf16[160,1024]{1,0:T(8,128)(2,1)} copy(bf16[160,1024]{1,0:T(8,128)(2,1)} %hyena_block.1) | data formatting | bytes 655360
